TPU v7x, 32 devices: a whole 2x2x4 slice. The times are simulated.
32 devices in a mesh: band: 4 (over z), sector: 8 (over y, x, core).
Axes of the slice: x: 2, y: 2, z: 4, core: 2. Of those that a mesh axis runs over, the one named last changes fastest.
Arguments:
- node_states: bfloat16 [16, 128, 512], P('band', 'sector'), may hold values from -6 to 6
- edge_states: bfloat16 [32, 512, 512], P(('band', 'sector')), may hold values from -6 to 6
- senders: int32 [32, 512], P(('band', 'sector')), may hold values from 0 to 351, as said below
- receivers: int32 [32, 512], P(('band', 'sector')), may hold values from 0 to 63
- edge_count: int32 [32], P(('band', 'sector')), may hold values from 128 to 512, as said below
- edge_hidden: bfloat16 [2, 1536, 512], replicated, may hold values from -0.15625 to 0.15625
- edge_offset: float32 [2, 512], replicated, may hold values from -3 to 3
- edge_output: bfloat16 [2, 512, 512], replicated, may hold values from -0.25 to 0.25
- edge_scale: float32 [2, 512], replicated, may hold values from 0.5 to 1.5
- node_hidden: bfloat16 [2, 1024, 512], replicated, may hold values from -0.1875 to 0.1875
- node_offset: float32 [2, 512], replicated, may hold values from -3 to 3
- node_output: bfloat16 [2, 512, 512], replicated, may hold values from -0.25 to 0.25
- node_scale: float32 [2, 512], replicated, may hold values from 0.5 to 1.5
- output_cotangent: bfloat16 [16, 128, 512], P('band', 'sector'), may hold values from -6 to 6
Outputs:
- node_result: bfloat16 [16, 128, 512], P('band', 'sector')
- node_gradient: float32 [16, 128, 512], P('band', 'sector')
- edge_gradient: float32 [32, 512, 512], P(('band', 'sector'))
- edge_hidden_gradient: float32 [2, 1536, 512], replicated
- edge_offset_gradient: float32 [2, 512], replicated
- edge_output_gradient: float32 [2, 512, 512], replicated
- edge_scale_gradient: float32 [2, 512], replicated
- node_hidden_gradient: float32 [2, 1024, 512], replicated
- node_offset_gradient: float32 [2, 512], replicated
- node_output_gradient: float32 [2, 512, 512], replicated
- node_scale_gradient: float32 [2, 512], replicated
Inputs may be any that keep to these rules, and one draw needn't show every extreme that they name: `senders`: an entry below 288 names a cell of the device's extended block (row-major, 12 rows); devices of the first band never name its first 4 rows, devices of the last band never its last 4 rows. An entry 288 + c names coarse node c. `edge_count`: slots at or past a device's count hold no edge. Some device has all 512 slots live.
All inputs are finite; a program needn't handle non-finite values.
Results may differ from a plain program's by a relative error of at most 0.019.
Values may be sent and summed in bfloat16 or wider, within the bound.
No kernel may reach another device: no remote copies, remote signals or barrier semaphores. Data moves between devices by JAX's collectives and lax.ppermute only.
A program may use at most 128 MiB of HBM per device.

v0:
```python
import math
import jax
import jax.numpy as jnp
from jax import lax
from jax.sharding import PartitionSpec as P

CO = 2
epsilon = 1e-05


def shifted(shard, axis, by):
    length = lax.axis_size(axis)
    return lax.ppermute(shard, axis, [(i, (i + by) % length) for i in range(length)])


def passed_along(block, axis, distance):
    devices = range(lax.axis_size(axis))
    route = [(i - distance, i) for i in devices if i - distance in devices]
    return lax.ppermute(block, axis, route)


def extended_2(cells, sides, width):
    for axis, dim in sides:
        count = lax.axis_size(axis)
        head = lax.slice_in_dim(cells, 0, width, axis=dim)
        tail = lax.slice_in_dim(cells, cells.shape[dim] - width, cells.shape[dim], axis=dim)
        cells = jnp.concatenate(
            [
                lax.ppermute(tail, axis, [(i, (i + 1) % count) for i in range(count)]),
                cells,
                lax.ppermute(head, axis, [((i + 1) % count, i) for i in range(count)]),
            ],
            axis=dim,
        )
    return cells


def mlp_forward(inputs, first_weight, first_bias, second_weight, norm_gain):
    pre_act = jnp.dot(inputs, first_weight, preferred_element_type=jnp.float32) + first_bias
    sigmoid_val = jax.nn.sigmoid(pre_act)
    activated = (pre_act * sigmoid_val).astype(jnp.bfloat16)
    mixed = jnp.dot(activated, second_weight, preferred_element_type=jnp.float32)
    centered = mixed - jnp.mean(mixed, axis=-1, keepdims=True)
    inv_std = lax.rsqrt(jnp.mean(centered * centered, axis=-1, keepdims=True) + epsilon)
    normed = centered * inv_std
    return (normed * norm_gain, (inputs, pre_act, sigmoid_val, activated, normed, inv_std))


def mlp_backward(grad_out, saved, first_weight, second_weight, norm_gain):
    inputs, pre_act, sigmoid_val, activated, normed, inv_std = saved
    grad_gain = jnp.sum(grad_out * normed, axis=0)
    grad_normed = grad_out * norm_gain
    grad_mixed = inv_std * (
        grad_normed
        - jnp.mean(grad_normed, axis=-1, keepdims=True)
        - normed * jnp.mean(grad_normed * normed, axis=-1, keepdims=True)
    )
    mixed_low = grad_mixed.astype(jnp.bfloat16)
    grad_second = lax.dot_general(
        activated, mixed_low, (((0,), (0,)), ((), ())), preferred_element_type=jnp.float32
    )
    grad_act = lax.dot_general(
        mixed_low, second_weight, (((1,), (1,)), ((), ())), preferred_element_type=jnp.float32
    )
    grad_pre = grad_act * sigmoid_val * (1.0 + pre_act * (1.0 - sigmoid_val))
    grad_bias = jnp.sum(grad_pre, axis=0)
    pre_low = grad_pre.astype(jnp.bfloat16)
    grad_first = lax.dot_general(
        inputs, pre_low, (((0,), (0,)), ((), ())), preferred_element_type=jnp.float32
    )
    grad_inputs = lax.dot_general(
        pre_low, first_weight, (((1,), (1,)), ((), ())), preferred_element_type=jnp.float32
    )
    return (grad_inputs, (grad_first, grad_bias, grad_second, grad_gain))


def fold_sector(grad_block, reach):
    kept = grad_block.shape[1] - 2 * reach
    middle = grad_block[:, reach : reach + kept]
    from_next = shifted(grad_block[:, :reach].astype(jnp.bfloat16), "sector", -1).astype(
        jnp.float32
    )
    from_prev = shifted(grad_block[:, reach + kept :].astype(jnp.bfloat16), "sector", 1).astype(
        jnp.float32
    )
    return middle.at[:, kept - reach :].add(from_next).at[:, :reach].add(from_prev)


def fold_band(grad_block, reach):
    kept = grad_block.shape[0] - 2 * reach
    middle = grad_block[reach : reach + kept]
    from_next = passed_along(grad_block[:reach].astype(jnp.bfloat16), "band", -1).astype(
        jnp.float32
    )
    from_prev = passed_along(grad_block[reach + kept :].astype(jnp.bfloat16), "band", 1).astype(
        jnp.float32
    )
    return middle.at[kept - reach :].add(from_next).at[:reach].add(from_prev)


def local(
    node_states,
    edge_states,
    senders,
    receivers,
    edge_count,
    edge_hidden,
    edge_offset,
    edge_output,
    edge_scale,
    node_hidden,
    node_offset,
    node_output,
    node_scale,
    output_cotangent,
):
    lat_rows, lon_cols, width = node_states.shape
    node_rows = lat_rows * lon_cols
    slots = edge_states.shape[1]
    depth = edge_hidden.shape[0]
    ext_rows = 3 * lat_rows * (lon_cols + 2 * lat_rows)
    table_rows = ext_rows + CO * lax.axis_size("band") * lax.axis_size("sector")
    edge_rows = edge_states[0]
    send_index = senders[0]
    recv_index = receivers[0]
    live_count = edge_count[0]
    live_mask = (jnp.arange(slots, dtype=jnp.int32) < live_count).astype(jnp.float32)[:, None]
    incidence = (recv_index[:, None] == jnp.arange(node_rows, dtype=jnp.int32)[None, :]).astype(
        jnp.float32
    )
    sender_onehot = (
        send_index[:, None] == jnp.arange(table_rows, dtype=jnp.int32)[None, :]
    ).astype(jnp.float32)
    state = node_states.reshape(node_rows, width)
    records = []
    for depth_index in range(depth):
        edge_params = (
            edge_hidden[depth_index],
            edge_offset[depth_index],
            edge_output[depth_index],
            edge_scale[depth_index],
        )
        node_params = (
            node_hidden[depth_index],
            node_offset[depth_index],
            node_output[depth_index],
            node_scale[depth_index],
        )
        extended = extended_2(
            state.reshape(lat_rows, lon_cols, width), (("band", 0), ("sector", 1)), lat_rows
        )
        coarse = lax.all_gather(state[:CO], ("band", "sector"), axis=0, tiled=True)
        table = jnp.concatenate([extended.reshape(ext_rows, width), coarse], axis=0)
        inputs = jnp.concatenate(
            [edge_rows, jnp.take(table, send_index, axis=0), jnp.take(state, recv_index, axis=0)],
            axis=1,
        )
        result, edge_saved = mlp_forward(
            inputs, edge_params[0], edge_params[1], edge_params[2], edge_params[3]
        )
        update = result * live_mask
        summed = lax.dot_general(
            incidence,
            update,
            (((0,), (0,)), ((), ())),
            precision=lax.Precision.HIGHEST,
            preferred_element_type=jnp.float32,
        )
        node_inputs = jnp.concatenate([state, summed.astype(jnp.bfloat16)], axis=1)
        node_delta, node_saved = mlp_forward(
            node_inputs, node_params[0], node_params[1], node_params[2], node_params[3]
        )
        records.append((inputs, edge_saved, node_saved))
        edge_rows = (edge_rows.astype(jnp.float32) + update).astype(jnp.bfloat16)
        state = (state.astype(jnp.float32) + node_delta).astype(jnp.bfloat16)
    node_result = state.reshape(lat_rows, lon_cols, width)
    grad_state = output_cotangent.reshape(node_rows, width).astype(jnp.float32)
    grad_edges = jnp.zeros((slots, width), jnp.float32)
    per_layer = [None] * depth
    for depth_index in reversed(range(depth)):
        inputs, edge_saved, node_saved = records[depth_index]
        edge_params = (
            edge_hidden[depth_index],
            edge_offset[depth_index],
            edge_output[depth_index],
            edge_scale[depth_index],
        )
        grad_in, node_grads = mlp_backward(
            grad_state,
            node_saved,
            node_hidden[depth_index],
            node_output[depth_index],
            node_scale[depth_index],
        )
        grad_state = grad_state + grad_in[:, :width]
        spread = jnp.dot(
            incidence,
            grad_in[:, width:],
            precision=lax.Precision.HIGHEST,
            preferred_element_type=jnp.float32,
        )
        flow_grad = (spread + grad_edges) * live_mask
        grad_inputs, edge_grads = mlp_backward(
            flow_grad, edge_saved, edge_params[0], edge_params[2], edge_params[3]
        )
        grad_edges = grad_edges + grad_inputs[:, :width]
        grad_state = grad_state + lax.dot_general(
            incidence,
            grad_inputs[:, 2 * width :],
            (((0,), (0,)), ((), ())),
            precision=lax.Precision.HIGHEST,
            preferred_element_type=jnp.float32,
        )
        table_grad = lax.dot_general(
            sender_onehot,
            grad_inputs[:, width : 2 * width],
            (((0,), (0,)), ((), ())),
            precision=lax.Precision.HIGHEST,
            preferred_element_type=jnp.float32,
        )
        ext_grad = table_grad[:ext_rows].reshape(3 * lat_rows, lon_cols + 2 * lat_rows, width)
        coarse_grad = table_grad[ext_rows:]
        returned = fold_band(fold_sector(ext_grad, lat_rows), lat_rows)
        grad_state = grad_state + returned.reshape(node_rows, width)
        layer_grads = edge_grads + node_grads
        summed_grads = lax.psum(
            (
                layer_grads[0],
                layer_grads[1],
                layer_grads[2],
                layer_grads[3],
                layer_grads[4],
                layer_grads[5],
                layer_grads[6],
                layer_grads[7],
                coarse_grad,
            ),
            ("band", "sector"),
        )
        own_coarse = lax.dynamic_slice_in_dim(
            summed_grads[8], lax.axis_index(("band", "sector")) * CO, CO, 0
        )
        per_layer[depth_index] = tuple(summed_grads[:8])
        grad_state = grad_state.at[:CO].add(own_coarse)
    stacked = [
        jnp.stack([per_layer[depth_index][item] for depth_index in range(depth)])
        for item in range(8)
    ]
    factor = 1.0 / math.sqrt(node_rows * lax.axis_size("band") * lax.axis_size("sector"))
    return (
        node_result,
        grad_state.reshape(lat_rows, lon_cols, width),
        grad_edges[None],
        stacked[0] * factor,
        stacked[1] * factor,
        stacked[2] * factor,
        stacked[3] * factor,
        stacked[4] * factor,
        stacked[5] * factor,
        stacked[6] * factor,
        stacked[7] * factor,
    )


def solution(mesh):
    return jax.shard_map(
        local,
        mesh=mesh,
        in_specs=(
            P("band", "sector", None),
            P(("band", "sector"), None, None),
            P(("band", "sector"), None),
            P(("band", "sector"), None),
            P(("band", "sector")),
            P(),
            P(),
            P(),
            P(),
            P(),
            P(),
            P(),
            P(),
            P("band", "sector", None),
        ),
        out_specs=(
            P("band", "sector", None),
            P("band", "sector", None),
            P(("band", "sector"), None, None),
            P(),
            P(),
            P(),
            P(),
            P(),
            P(),
            P(),
            P(),
        ),
        check_vma=False,
    )
```

profile of v0, /device:TPU:0, one launch (start us, length us, event | category | flops | bytes accessed | tf_op | source)
XLA Modules:
  0.0 573.9 jit_solution(11229786818335599624)
XLA Ops:
  7.3 3.1 collective-permute-start
  10.4 2.1 collective-permute-start.1
  15.3 2.9 gather_fusion.1
  22.3 39.2 %all-gather = bf16[32,2,512]{2,1,0:T(2,128)(2,1)S(1)} all-gather(bf16[1,2,512]{2,1,0:T(2,128)(2,1)S(1)} %slice_bitcast_fusion.1), channel_id=1, replica_groups=mesh['band'=4,'sector'=8] {'band','sector'}, dimensions={0}, use_global_device_ids=true | all-gather | bytes 67584 | tf_op jit(solution)/shard_map/all_gather | solution.py:152
  62.5 2.0 gather_fusion
  64.8 2.6 fusion.15
  70.5 2.0 gather_fusion.3
  72.6 2.0 collective-permute-start.4
  79.4 37.3 %all-gather.1 = bf16[32,2,512]{2,1,0:T(2,128)(2,1)S(1)} all-gather(bf16[1,2,512]{2,1,0:T(2,128)(2,1)S(1)} %slice_bitcast_fusion), channel_id=1, replica_groups=mesh['band'=4,'sector'=8] {'band','sector'}, dimensions={0}, use_global_device_ids=true | all-gather | bytes 67584 | tf_op jit(solution)/shard_map/all_gather | solution.py:152
  119.2 2.7 fusion.18
  132.9 2.7 convolution_bitcast_fusion
  145.1 3.2 collective-permute-done.9
  153.8 2.9 collective-permute-done.10
  158.5 109.4 %all-reduce.5.cloned.1.call-done = f32[64,512]{1,0:T(8,128)} async-done(((f32[64,512]{1,0:T(8,128)}), f32[64,512]{1,0:T(8,128)}) %all-reduce.5.cloned.1.call-update) | async-done | bytes 131088 | tf_op jit(solution)/shard_map/psum | solution.py:226
  277.2 2.7 convolution_bitcast_fusion.1
  290.1 2.5 copy.42
  292.6 42.0 %all-reduce = (f32[1,512]{1,0:T(1,128)S(1)}, f32[1,512]{1,0:T(1,128)S(1)}, f32[1,512]{1,0:T(1,128)S(1)}, f32[1,512]{1,0:T(1,128)S(1)}, f32[1,512]{1,0:T(1,128)S(...) all-reduce(f32[1,512]{1,0:T(1,128)S(1)} %bitcast.197, ...), channel_id=1, replica_groups=mesh['band'=4,'sector'=8] {'band','sector'}, use_global_device_ids=true, to_apply=%region_23.26 | all-reduce | flops 4096 | bytes 32768 | tf_op jit(solution)/shard_map/psum | solution.py:226
  335.8 2.8 add_bitcast_fusion
  340.1 2.5 copy.40
  346.9 2.5 collective-permute-start.15
  353.0 4.3 collective-permute-done.14
  359.7 193.0 %all-reduce.7.cloned.1.call-done = (f32[64,512]{1,0:T(8,128)}, f32[1,1536,512]{2,1,0:T(8,128)}, f32[1,1536,512]{2,1,0:T(8,128)}, f32[1,512,512]{2,1,0:T(8,128)},...) async-done(((f32[64,512]{1,0:T(8,128)}, f32[1,1536,512]{2,1,0:T(8,128)}, ...) | async-done | bytes 14811152 | tf_op jit(solution)/shard_map/psum | solution.py:226
  553.5 6.5 %maximum_multiply_fusion = f32[2,1536,512]{2,1,0:T(8,128)} fusion(f32[1,1536,512]{2,1,0:T(8,128)} %get-tuple-element.207, f32[1,1536,512]{2,1,0:T(8,128)} %get-tuple-element.208), kind=kLoop, calls=%fused_computation.4 | loop fusion | flops 3145728 | bytes 12582912 | tf_op jit(solution)/shard_map/mul | solution.py:254
  563.0 2.5 maximum_multiply_fusion.1
  (280 shorter events, 82.6 us)
Async XLA Ops:
  7.2 260.8 %all-reduce.5.cloned.1.call-start = ((), (), s32[]{:S(2)}) async-start(), calls=%async_computation | async-start | bytes 262144 | tf_op jit(solution)/shard_map/psum | solution.py:226
  7.3 13.2 %collective-permute-start = (bf16[4,16,512]{2,1,0:T(8,128)(2,1)}, bf16[4,16,512]{2,1,0:T(8,128)(2,1)S(1)}, u32[]{:S(2)}, u32[]{:S(2)}) collective-permute-start(bf16[4,16,512]{2,1,0:T(8,128)(2,1)} %param.46), channel_id=1, source_target_pairs={{0,8},{8,16},{16,24},{24,0},{1,9},{9,17},{17,25},{25,1},{2,10},{10... | collective-permute-start | bytes 196616 | tf_op jit(solution)/shard_map/ppermute | solution.py:29
  10.4 10.1 %collective-permute-start.1 = (bf16[4,16,512]{2,1,0:T(8,128)(2,1)}, bf16[4,16,512]{2,1,0:T(8,128)(2,1)S(1)}, u32[]{:S(2)}, u32[]{:S(2)}) collective-permute-start(bf16[4,16,512]{2,1,0:T(8,128)(2,1)} %param.46), channel_id=1, source_target_pairs={{8,0},{16,8},{24,16},{0,24},{9,1},{17,9},{25,17},{1,25},{10,2},{18... | collective-permute-start | bytes 196616 | tf_op jit(solution)/shard_map/ppermute | solution.py:31
  19.7 54.9 %copy-start.35 = (f32[1,512]{1,0:T(1,128)}, f32[1,512]{1,0:T(1,128)S(1)}, u32[]{:S(2)}) copy-start(f32[1,512]{1,0:T(1,128)S(1)} %get-tuple-element.234) | copy-start | bytes 6148
  20.6 41.8 %collective-permute-start.3 = (bf16[12,4,512]{2,1,0:T(4,128)(2,1)S(1)}, bf16[12,4,512]{2,1,0:T(4,128)(2,1)S(1)}, u32[]{:S(2)}, u32[]{:S(2)}) collective-permute-start(bf16[12,4,512]{2,1,0:T(4,128)(2,1)S(1)} %get-tuple-element.226), channel_id=1, source_target_pairs={{1,0},{2,1},{3,2},{4,3},{5,4},{6,5},{7,6},{0,7},{9,8},{10,9},{11,1... | collective-permute-start | bytes 147464 | tf_op jit(solution)/shard_map/ppermute | solution.py:31
  22.2 40.1 %collective-permute-start.2 = (bf16[12,4,512]{2,1,0:T(4,128)(2,1)S(1)}, bf16[12,4,512]{2,1,0:T(4,128)(2,1)S(1)}, u32[]{:S(2)}, u32[]{:S(2)}) collective-permute-start(bf16[12,4,512]{2,1,0:T(4,128)(2,1)S(1)} %get-tuple-element.225), channel_id=1, source_target_pairs={{0,1},{1,2},{2,3},{3,4},{4,5},{5,6},{6,7},{7,0},{8,9},{9,10},{10,1... | collective-permute-start | bytes 147464 | tf_op jit(solution)/shard_map/ppermute | solution.py:29
  72.5 4.4 collective-permute-start.5
  72.6 6.2 %collective-permute-start.4 = (bf16[4,16,512]{2,1,0:T(8,128)(2,1)S(1)}, bf16[4,16,512]{2,1,0:T(8,128)(2,1)S(1)}, u32[]{:S(2)}, u32[]{:S(2)}) collective-permute-start(bf16[4,16,512]{2,1,0:T(8,128)(2,1)S(1)} %bitcast.142), channel_id=1, source_target_pairs={{0,8},{8,16},{16,24},{24,0},{1,9},{9,17},{17,25},{25,1},{2,10},{10... | collective-permute-start | bytes 196616 | tf_op jit(solution)/shard_map/ppermute | solution.py:29
  78.8 37.9 %collective-permute-start.7 = (bf16[12,4,512]{2,1,0:T(4,128)(2,1)S(1)}, bf16[12,4,512]{2,1,0:T(4,128)(2,1)S(1)}, u32[]{:S(2)}, u32[]{:S(2)}) collective-permute-start(bf16[12,4,512]{2,1,0:T(4,128)(2,1)S(1)} %get-tuple-element.224), channel_id=1, source_target_pairs={{1,0},{2,1},{3,2},{4,3},{5,4},{6,5},{7,6},{0,7},{9,8},{10,9},{11,1... | collective-permute-start | bytes 147464 | tf_op jit(solution)/shard_map/ppermute | solution.py:31
  78.9 37.9 %collective-permute-start.6 = (bf16[12,4,512]{2,1,0:T(4,128)(2,1)S(1)}, bf16[12,4,512]{2,1,0:T(4,128)(2,1)S(1)}, u32[]{:S(2)}, u32[]{:S(2)}) collective-permute-start(bf16[12,4,512]{2,1,0:T(4,128)(2,1)S(1)} %get-tuple-element.223), channel_id=1, source_target_pairs={{0,1},{1,2},{2,3},{3,4},{4,5},{5,6},{6,7},{7,0},{8,9},{9,10},{10,1... | collective-permute-start | bytes 147464 | tf_op jit(solution)/shard_map/ppermute | solution.py:29
  138.9 5.3 collective-permute-start.8
  143.5 129.1 %copy-start.2 = (f32[512,512]{0,1:T(8,128)}, f32[512,512]{0,1:T(8,128)S(1)}, u32[]{:S(2)}) copy-start(f32[512,512]{0,1:T(8,128)S(1)} %copy.41) | copy-start | bytes 3145732
  143.5 4.8 collective-permute-start.9
  144.1 408.6 %all-reduce.7.cloned.1.call-start = ((), (), s32[]{:S(2)}) async-start(), calls=%async_computation.1 | async-start | bytes 29622272 | tf_op jit(solution)/shard_map/psum | solution.py:226
  145.1 124.5 %copy-start.30 = (f32[64,512]{1,0:T(8,128)S(1)}, f32[64,512]{1,0:T(8,128)}, u32[]{:S(2)}) copy-start(f32[64,512]{1,0:T(8,128)} %copy-done.29) | copy-start | bytes 393220
  149.2 4.6 collective-permute-start.11
  150.5 6.2 %collective-permute-start.10 = (bf16[4,16,512]{2,1,0:T(8,128)(2,1)S(1)}, bf16[4,16,512]{2,1,0:T(8,128)(2,1)S(1)}, u32[]{:S(2)}, u32[]{:S(2)}) collective-permute-start(bf16[4,16,512]{2,1,0:T(8,128)(2,1)S(1)} %get-tuple-element.221), channel_id=1, source_target_pairs={{8,0},{16,8},{24,16},{9,1},{17,9},{25,17},{10,2},{18,10},{26,18},{... | collective-permute-start | bytes 196616 | tf_op jit(solution)/shard_map/ppermute | solution.py:19
  153.8 118.8 %copy-start.36 = (f32[1,512]{1,0:T(1,128)S(1)}, f32[1,512]{1,0:T(1,128)}, u32[]{:S(2)}) copy-start(f32[1,512]{1,0:T(1,128)} %copy-done.35) | copy-start | bytes 6148
  153.8 118.8 %copy-start.38 = (f32[512]{0:T(512)S(1)}, f32[512]{0:T(512)}, u32[]{:S(2)}) copy-start(f32[512]{0:T(512)} %copy-done.37) | copy-start | bytes 6148
  153.8 118.9 %copy-start.42 = (f32[512]{0:T(512)S(1)}, f32[512]{0:T(512)}, u32[]{:S(2)}) copy-start(f32[512]{0:T(512)} %copy-done.40) | copy-start | bytes 6148
  289.5 53.1 %collective-permute-start.12 = (bf16[12,4,512]{2,1,0:T(4,128)(2,1)S(1)}, bf16[12,4,512]{2,1,0:T(4,128)(2,1)S(1)}, u32[]{:S(2)}, u32[]{:S(2)}) collective-permute-start(bf16[12,4,512]{2,1,0:T(4,128)(2,1)S(1)} %get-tuple-element.216), channel_id=1, source_target_pairs={{0,7},{1,0},{2,1},{3,2},{4,3},{5,4},{6,5},{7,6},{8,15},{9,8},{10,9... | collective-permute-start | bytes 147464 | tf_op jit(solution)/shard_map/ppermute | solution.py:13
  289.7 54.5 %collective-permute-start.13 = (bf16[12,4,512]{2,1,0:T(4,128)(2,1)S(1)}, bf16[12,4,512]{2,1,0:T(4,128)(2,1)S(1)}, u32[]{:S(2)}, u32[]{:S(2)}) collective-permute-start(bf16[12,4,512]{2,1,0:T(4,128)(2,1)S(1)} %get-tuple-element.215), channel_id=1, source_target_pairs={{0,1},{1,2},{2,3},{3,4},{4,5},{5,6},{6,7},{7,0},{8,9},{9,10},{10,1... | collective-permute-start | bytes 147464 | tf_op jit(solution)/shard_map/ppermute | solution.py:13
  346.9 6.0 %collective-permute-start.15 = (bf16[4,16,512]{2,1,0:T(8,128)(2,1)S(1)}, bf16[4,16,512]{2,1,0:T(8,128)(2,1)S(1)}, u32[]{:S(2)}, u32[]{:S(2)}) collective-permute-start(bf16[4,16,512]{2,1,0:T(8,128)(2,1)S(1)} %get-tuple-element.220), channel_id=1, source_target_pairs={{0,8},{8,16},{16,24},{1,9},{9,17},{17,25},{2,10},{10,18},{18,26},{... | collective-permute-start | bytes 196616 | tf_op jit(solution)/shard_map/ppermute | solution.py:19
  349.4 7.8 %collective-permute-start.14 = (bf16[4,16,512]{2,1,0:T(8,128)(2,1)S(1)}, bf16[4,16,512]{2,1,0:T(8,128)(2,1)S(1)}, u32[]{:S(2)}, u32[]{:S(2)}) collective-permute-start(bf16[4,16,512]{2,1,0:T(8,128)(2,1)S(1)} %get-tuple-element.219), channel_id=1, source_target_pairs={{8,0},{16,8},{24,16},{9,1},{17,9},{25,17},{10,2},{18,10},{26,18},{... | collective-permute-start | bytes 196616 | tf_op jit(solution)/shard_map/ppermute | solution.py:19
  (59 other events, 374.0 us)
Sparse Core Ops, SparseCore 0:
  144.2 123.7 all-reduce.4
  287.2 265.4 all-reduce.6
where the time goes:
time: 575 us; the launch traced here: 574 us
  waiting for transfers between devices  317 us (55%)
  blocking collectives  118 us (21%)
  matrix products  40.5 us (7%)
  other arithmetic  33.4 us (6%)
  local copies, waits for them, and re-layouts  31 us (5%)
  starting transfers between devices  17.3 us (3%)
  between operations  15.9 us (3%)
    psum x2, waiting for transfers between devices, local(): lax.psum((layer_grads[0], layer_grads[1], layer_grads[2], layer_grads[3],...  302 us
    all_gather x2, blocking collectives, local(): coarse = lax.all_gather(state[:CO], ('band', 'sector'), axis=0, tiled=True)  76.5 us
    psum x1, blocking collectives, local(): lax.psum((layer_grads[0], layer_grads[1], layer_grads[2], layer_grads[3],...  42 us
    unnamed x140, local copies, waits for them, and re-layouts  13.2 us
  transfers between devices with their start and end apart: 18, of which 8 were waited for; matrix products, arithmetic and copies ran while one was open for 7% of the time, Pallas kernels for 0%

commit v1 on v0

--- a/solution.py
+++ b/solution.py
@@ -223,20 +223,19 @@
         returned = fold_band(fold_sector(ext_grad, lat_rows), lat_rows)
         grad_state = grad_state + returned.reshape(node_rows, width)
         layer_grads = edge_grads + node_grads
-        summed_grads = lax.psum(
-            (
-                layer_grads[0],
-                layer_grads[1],
-                layer_grads[2],
-                layer_grads[3],
-                layer_grads[4],
-                layer_grads[5],
-                layer_grads[6],
-                layer_grads[7],
-                coarse_grad,
-            ),
-            ("band", "sector"),
-        )
+        summed_grads = (
+            layer_grads[0],
+            layer_grads[1],
+            layer_grads[2],
+            layer_grads[3],
+            layer_grads[4],
+            layer_grads[5],
+            layer_grads[6],
+            layer_grads[7],
+            coarse_grad,
+        )
+        for over in ("sector", "band"):
+            summed_grads = lax.psum(summed_grads, over)
         own_coarse = lax.dynamic_slice_in_dim(
             summed_grads[8], lax.axis_index(("band", "sector")) * CO, CO, 0
         )

time: 575 us -> 973 us (1.69)
  waiting for transfers between devices: 317 us -> 709 us
    psum x2 -> x4, waiting for transfers between devices: 302 us -> 695 us  [local(): summed_grads = lax.psum(summed_grads, over)]
    psum x1 -> x2, blocking collectives: 42 us -> 49.7 us  [local(): summed_grads = lax.psum(summed_grads, over)]
  transfers between devices with their start and end apart: 18 -> 20, of which waited for: 8 -> 9; matrix products, arithmetic and copies ran while one was open for 7% -> 4% of each run, Pallas kernels for 0% -> 0%
where the time goes in v1:
time: 973 us; the launch traced here: 972 us
  waiting for transfers between devices  709 us (73%)
  blocking collectives  126 us (13%)
  matrix products  42.1 us (4%)
  other arithmetic  33.3 us (3%)
  local copies, waits for them, and re-layouts  29.2 us (3%)
  starting transfers between devices  16.8 us (2%)
  between operations  15.6 us (2%)
    psum x4, waiting for transfers between devices, local(): summed_grads = lax.psum(summed_grads, over)  695 us
    all_gather x2, blocking collectives, local(): coarse = lax.all_gather(state[:CO], ('band', 'sector'), axis=0, tiled=True)  76.5 us
    psum x2, blocking collectives, local(): summed_grads = lax.psum(summed_grads, over)  49.7 us
  transfers between devices with their start and end apart: 20, of which 9 were waited for; matrix products, arithmetic and copies ran while one was open for 4% of the time, Pallas kernels for 0%

profile of v1, /device:TPU:0, one launch (start us, length us, event | category | flops | bytes accessed | tf_op | source)
XLA Modules:
  0.0 972.0 jit_solution(6243084011863799762)
XLA Ops:
  7.3 3.1 collective-permute-start
  10.4 2.1 collective-permute-start.1
  15.3 2.9 gather_fusion.1
  22.3 39.2 %all-gather = bf16[32,2,512]{2,1,0:T(2,128)(2,1)S(1)} all-gather(bf16[1,2,512]{2,1,0:T(2,128)(2,1)S(1)} %slice_bitcast_fusion.1), channel_id=1, replica_groups=mesh['band'=4,'sector'=8] {'band','sector'}, dimensions={0}, use_global_device_ids=true | all-gather | bytes 67584 | tf_op jit(solution)/shard_map/all_gather | solution.py:152
  64.8 2.6 fusion.15
  72.6 2.0 collective-permute-start.4
  79.4 37.3 %all-gather.1 = bf16[32,2,512]{2,1,0:T(2,128)(2,1)S(1)} all-gather(bf16[1,2,512]{2,1,0:T(2,128)(2,1)S(1)} %slice_bitcast_fusion), channel_id=1, replica_groups=mesh['band'=4,'sector'=8] {'band','sector'}, dimensions={0}, use_global_device_ids=true | all-gather | bytes 67584 | tf_op jit(solution)/shard_map/all_gather | solution.py:152
  119.3 2.7 fusion.18
  132.9 2.7 fusion.41
  142.8 3.2 collective-permute-done.9
  149.4 2.2 fusion.117
  152.0 42.7 %all-reduce.9.cloned.1.call-done = f32[64,512]{1,0:T(8,128)} async-done(((f32[64,512]{1,0:T(8,128)}), f32[64,512]{1,0:T(8,128)}) %all-reduce.9.cloned.1.call-update) | async-done | bytes 131088 | tf_op jit(solution)/shard_map/psum | solution.py:238
  197.8 33.3 %all-reduce.11.cloned.1.call-done = f32[64,512]{1,0:T(8,128)} async-done(((f32[64,512]{1,0:T(8,128)}), f32[64,512]{1,0:T(8,128)}) %all-reduce.11.cloned.1.call-update) | async-done | bytes 131088 | tf_op jit(solution)/shard_map/psum | solution.py:238
  241.0 2.7 fusion.42
  250.9 196.4 %all-reduce.13.cloned.1.call-done = (f32[64,512]{1,0:T(8,128)}, f32[1536,512]{1,0:T(8,128)}, f32[1536,512]{1,0:T(8,128)}, f32[512,512]{1,0:T(8,128)}, f32[512,51...) async-done(((f32[64,512]{1,0:T(8,128)}, f32[1536,512]{1,0:T(8,128)}, f32[1536,512]{1,0:T(8,128)}, ...) | async-done | bytes 14811152 | tf_op jit(solution)/shard_map/psum | solution.py:238
  451.0 2.5 copy.42
  453.5 26.1 %all-reduce = (f32[512]{0:T(512)S(1)}, f32[512]{0:T(512)S(1)}, f32[512]{0:T(512)S(1)}, f32[512]{0:T(512)S(1)}, f32[512]{0:T(512)S(1)}, /*index=5*/f32[512]{0:T(512)S(1)}, f32[512]{0:T(512)S(1)}, f32[512]{0:T(512)S(1)}) all-reduce(f32[512]{0:T(512)S(1)} %copy-done.57, ...), channel_id=1, replica_groups=mesh['band'=4,'sector'=8] {'sector'}, use_global_device_ids=true, to_apply=%region_28.31 | all-reduce | flops 4096 | bytes 32768 | tf_op jit(solution)/shard_map/psum | solution.py:238
  479.6 23.6 %all-reduce.2 = (f32[1,512]{1,0:T(1,128)S(1)}, f32[1,512]{1,0:T(1,128)S(1)}, f32[1,512]{1,0:T(1,128)S(1)}, f32[1,512]{1,0:T(1,128)S(1)}, f32[1,512]{1,0:T(1,128)...) all-reduce(f32[1,512]{1,0:T(1,128)S(1)} %bitcast.192, ...), channel_id=1, replica_groups=mesh['band'=4,'sector'=8] {'band'}, use_global_device_ids=true, to_apply=%region_29.32 | all-reduce | flops 4096 | bytes 32768 | tf_op jit(solution)/shard_map/psum | solution.py:238
  504.4 2.7 add_bitcast_fusion
  508.5 2.5 copy.40
  519.9 6.2 collective-permute-done.14
  528.5 422.7 %all-reduce.15.cloned.1.call-done = (f32[64,512]{1,0:T(8,128)}, f32[1,1536,512]{2,1,0:T(8,128)}, f32[1,1536,512]{2,1,0:T(8,128)}, f32[1,512,512]{2,1,0:T(8,128)}...) async-done(((f32[64,512]{1,0:T(8,128)}, f32[1,1536,512]{2,1,0:T(8,128)}, ...) | async-done | bytes 14811152 | tf_op jit(solution)/shard_map/psum | solution.py:238
  951.9 6.5 maximum_multiply_fusion
  961.4 2.5 maximum_multiply_fusion.1
  (288 shorter events, 86.0 us)
Async XLA Ops:
  7.2 187.5 %all-reduce.9.cloned.1.call-start = ((), (), s32[]{:S(2)}) async-start(), calls=%async_computation | async-start | bytes 262144 | tf_op jit(solution)/shard_map/psum | solution.py:238
  7.3 13.2 %collective-permute-start = (bf16[4,16,512]{2,1,0:T(8,128)(2,1)}, bf16[4,16,512]{2,1,0:T(8,128)(2,1)S(1)}, u32[]{:S(2)}, u32[]{:S(2)}) collective-permute-start(bf16[4,16,512]{2,1,0:T(8,128)(2,1)} %param.46), channel_id=1, source_target_pairs={{0,8},{8,16},{16,24},{24,0},{1,9},{9,17},{17,25},{25,1},{2,10},{10... | collective-permute-start | bytes 196616 | tf_op jit(solution)/shard_map/ppermute | solution.py:29
  10.4 10.1 %collective-permute-start.1 = (bf16[4,16,512]{2,1,0:T(8,128)(2,1)}, bf16[4,16,512]{2,1,0:T(8,128)(2,1)S(1)}, u32[]{:S(2)}, u32[]{:S(2)}) collective-permute-start(bf16[4,16,512]{2,1,0:T(8,128)(2,1)} %param.46), channel_id=1, source_target_pairs={{8,0},{16,8},{24,16},{0,24},{9,1},{17,9},{25,17},{1,25},{10,2},{18... | collective-permute-start | bytes 196616 | tf_op jit(solution)/shard_map/ppermute | solution.py:31
  13.9 50.9 %copy-start.46 = (pred[512]{0:T(512)(128)(4,1)}, pred[512]{0:T(512)(128)(4,1)S(1)}, u32[]{:S(2)}) copy-start(pred[512]{0:T(512)(128)(4,1)S(1)} %get-tuple-element.273) | copy-start | bytes 1540
  15.3 46.2 %copy-start.22 = (bf16[1,512,512]{2,1,0:T(8,128)(2,1)S(1)}, bf16[1,512,512]{2,1,0:T(8,128)(2,1)}, u32[]{:S(2)}) copy-start(bf16[1,512,512]{2,1,0:T(8,128)(2,1)} %param.47) | copy-start | bytes 1572868
  20.6 41.8 %collective-permute-start.3 = (bf16[12,4,512]{2,1,0:T(4,128)(2,1)S(1)}, bf16[12,4,512]{2,1,0:T(4,128)(2,1)S(1)}, u32[]{:S(2)}, u32[]{:S(2)}) collective-permute-start(bf16[12,4,512]{2,1,0:T(4,128)(2,1)S(1)} %get-tuple-element.243), channel_id=1, source_target_pairs={{1,0},{2,1},{3,2},{4,3},{5,4},{6,5},{7,6},{0,7},{9,8},{10,9},{11,1... | collective-permute-start | bytes 147464 | tf_op jit(solution)/shard_map/ppermute | solution.py:31
  22.2 40.1 %collective-permute-start.2 = (bf16[12,4,512]{2,1,0:T(4,128)(2,1)S(1)}, bf16[12,4,512]{2,1,0:T(4,128)(2,1)S(1)}, u32[]{:S(2)}, u32[]{:S(2)}) collective-permute-start(bf16[12,4,512]{2,1,0:T(4,128)(2,1)S(1)} %get-tuple-element.242), channel_id=1, source_target_pairs={{0,1},{1,2},{2,3},{3,4},{4,5},{5,6},{6,7},{7,0},{8,9},{9,10},{10,1... | collective-permute-start | bytes 147464 | tf_op jit(solution)/shard_map/ppermute | solution.py:29
  22.2 105.1 %copy-start.40 = (f32[512]{0:T(512)}, f32[512]{0:T(512)S(1)}, u32[]{:S(2)}) copy-start(f32[512]{0:T(512)S(1)} %fusion.107) | copy-start | bytes 6148
  72.5 4.4 collective-permute-start.5
  72.6 6.2 collective-permute-start.4
  78.8 38.0 %collective-permute-start.7 = (bf16[12,4,512]{2,1,0:T(4,128)(2,1)S(1)}, bf16[12,4,512]{2,1,0:T(4,128)(2,1)S(1)}, u32[]{:S(2)}, u32[]{:S(2)}) collective-permute-start(bf16[12,4,512]{2,1,0:T(4,128)(2,1)S(1)} %get-tuple-element.241), channel_id=1, source_target_pairs={{1,0},{2,1},{3,2},{4,3},{5,4},{6,5},{7,6},{0,7},{9,8},{10,9},{11,1... | collective-permute-start | bytes 147464 | tf_op jit(solution)/shard_map/ppermute | solution.py:31
  78.9 37.9 %collective-permute-start.6 = (bf16[12,4,512]{2,1,0:T(4,128)(2,1)S(1)}, bf16[12,4,512]{2,1,0:T(4,128)(2,1)S(1)}, u32[]{:S(2)}, u32[]{:S(2)}) collective-permute-start(bf16[12,4,512]{2,1,0:T(4,128)(2,1)S(1)} %get-tuple-element.240), channel_id=1, source_target_pairs={{0,1},{1,2},{2,3},{3,4},{4,5},{5,6},{6,7},{7,0},{8,9},{9,10},{10,1... | collective-permute-start | bytes 147464 | tf_op jit(solution)/shard_map/ppermute | solution.py:29
  138.9 3.1 collective-permute-start.8
  141.4 4.6 collective-permute-start.9
  141.9 89.2 %all-reduce.11.cloned.1.call-start = ((), (), s32[]{:S(2)}) async-start(), calls=%async_computation.1 | async-start | bytes 262144 | tf_op jit(solution)/shard_map/psum | solution.py:238
  146.8 48.2 %collective-permute-start.11 = (bf16[4,16,512]{2,1,0:T(8,128)(2,1)}, bf16[4,16,512]{2,1,0:T(8,128)(2,1)S(1)}, u32[]{:S(2)}, u32[]{:S(2)}) collective-permute-start(bf16[4,16,512]{2,1,0:T(8,128)(2,1)} %get-tuple-element.239), channel_id=1, source_target_pairs={{0,8},{8,16},{16,24},{1,9},{9,17},{17,25},{2,10},{10,18},{18,26},{... | collective-permute-start | bytes 196616 | tf_op jit(solution)/shard_map/ppermute | solution.py:19
  148.1 46.9 %collective-permute-start.10 = (bf16[4,16,512]{2,1,0:T(8,128)(2,1)}, bf16[4,16,512]{2,1,0:T(8,128)(2,1)S(1)}, u32[]{:S(2)}, u32[]{:S(2)}) collective-permute-start(bf16[4,16,512]{2,1,0:T(8,128)(2,1)} %get-tuple-element.238), channel_id=1, source_target_pairs={{8,0},{16,8},{24,16},{9,1},{17,9},{25,17},{10,2},{18,10},{26,18},{... | collective-permute-start | bytes 196616 | tf_op jit(solution)/shard_map/ppermute | solution.py:19
  152.0 85.8 %copy-start.2 = (f32[512,512]{0,1:T(8,128)}, f32[512,512]{0,1:T(8,128)S(1)}, u32[]{:S(2)}) copy-start(f32[512,512]{0,1:T(8,128)S(1)} %copy.41) | copy-start | bytes 3145732
  194.7 252.6 %all-reduce.13.cloned.1.call-start = ((), (), s32[]{:S(2)}) async-start(), calls=%async_computation.2 | async-start | bytes 29622272 | tf_op jit(solution)/shard_map/psum | solution.py:238
  250.9 700.3 %all-reduce.15.cloned.1.call-start = ((), (), s32[]{:S(2)}) async-start(), calls=%async_computation.3 | async-start | bytes 29622272 | tf_op jit(solution)/shard_map/psum | solution.py:238
  449.7 61.4 %collective-permute-start.12 = (bf16[12,4,512]{2,1,0:T(4,128)(2,1)S(1)}, bf16[12,4,512]{2,1,0:T(4,128)(2,1)S(1)}, u32[]{:S(2)}, u32[]{:S(2)}) collective-permute-start(bf16[12,4,512]{2,1,0:T(4,128)(2,1)S(1)} %get-tuple-element.233), channel_id=1, source_target_pairs={{0,7},{1,0},{2,1},{3,2},{4,3},{5,4},{6,5},{7,6},{8,15},{9,8},{10,9... | collective-permute-start | bytes 147464 | tf_op jit(solution)/shard_map/ppermute | solution.py:13
  451.0 61.7 %collective-permute-start.13 = (bf16[12,4,512]{2,1,0:T(4,128)(2,1)S(1)}, bf16[12,4,512]{2,1,0:T(4,128)(2,1)S(1)}, u32[]{:S(2)}, u32[]{:S(2)}) collective-permute-start(bf16[12,4,512]{2,1,0:T(4,128)(2,1)S(1)} %get-tuple-element.232), channel_id=1, source_target_pairs={{0,1},{1,2},{2,3},{3,4},{4,5},{5,6},{6,7},{7,0},{8,9},{9,10},{10,1... | collective-permute-start | bytes 147464 | tf_op jit(solution)/shard_map/ppermute | solution.py:13
  515.3 4.6 collective-permute-start.15
  516.6 9.4 collective-permute-start.14
  (62 other events, 298.2 us)
Sparse Core Ops, SparseCore 0:
  142.0 52.6 all-reduce.8
  197.0 34.0 all-reduce.10
  251.0 196.2 all-reduce.12
  450.9 500.2 all-reduce.14
